TPU v7x, 32 devices: a whole 2x2x4 slice. The times are simulated.
32 devices in a mesh: sub: 16 (over z, y, x), mode: 2 (over core).
Axes of the slice: x: 2, y: 2, z: 4, core: 2. Of those that a mesh axis runs over, the one named last changes fastest.
Arguments:
- coupling: bfloat16 [1024, 64, 128], P('sub'), may hold values from -0.5 to 0.5
- coupling_pairs: int32 [1024, 2], P('sub'), may hold values from 0 to 3, as said below
- modes: bfloat16 [1024, 256, 256], P('sub', None, 'mode'), may hold values from -6 to 6
- mode_weights: bfloat16 [1024, 256], P('sub', 'mode'), may hold values from 0 to 1, as said below
- parent_of: int32 [1024, 1], P('sub'), may hold values from 0 to 15; in each aligned block of 64 rows (0 to 63, 64 to 127, ...) at most 8 rows name the same one
- row_block: int32 [1024], P('sub'), may hold values from 0 to 7
- parent_modes: bfloat16 [16, 512, 256], P('sub'), may hold values from -1 to 1
- parent_eigs: float32 [16, 256], P('sub'), may hold values from 0.02 to 0.5
Outputs:
- strengths: float32 [1024, 256], P('sub', 'mode')
Inputs may be any that keep to these rules, and one draw needn't show every extreme that they name: `coupling_pairs`: within each child the 2 block indices are distinct. `parent_of`: the 64 children of one index of sub name any one parent at most 8 times; some parent is named exactly 8 times by some index's children. `mode_weights`: Positive.
All inputs are finite; a program needn't handle non-finite values.
Results may differ from a plain program's by a relative error of at most 0.0015.
Values may be sent and summed in bfloat16 or wider, within the bound.
A program may use at most 128 MiB of HBM per device.

v0:
```python
import jax
import jax.numpy as jnp
from jax import lax
from jax.sharding import PartitionSpec as P

M = 256
MP = 256
BLK = 64
CH_DEV = 64


def pick_blocks(modes, coupling_pairs):
    child_count, interface_rows, mode_cols = modes.shape
    blocks = modes.reshape(child_count, interface_rows // BLK, BLK, mode_cols)
    selector = (
        coupling_pairs[:, :, None]
        == jnp.arange(interface_rows // BLK, dtype=jnp.int32)[None, None, :]
    ).astype(jnp.bfloat16)
    picked = jnp.einsum(
        "skb,sbim->skim", selector, blocks, preferred_element_type=jnp.float32
    ).astype(jnp.bfloat16)
    return picked.reshape(child_count, coupling_pairs.shape[1] * BLK, mode_cols)


def weighted_records(coupling_rows, picked, weights):
    record = jnp.einsum("sij,sjm->sim", coupling_rows, picked, preferred_element_type=jnp.float32)
    return (record * weights[:, None, :].astype(jnp.float32)).astype(jnp.bfloat16)


def to_slots(values, slot_index, slot_count):
    empty = jnp.zeros((slot_count,) + values.shape[1:], values.dtype)
    return empty.at[slot_index].set(values)


def per_device(
    coupling, coupling_pairs, modes, mode_weights, parent_of, row_block, parent_modes, parent_eigs
):
    sub_count = lax.axis_size("sub")
    child_count = coupling.shape[0]
    mode_cols = modes.shape[2]
    capacity = max(2, 2 * child_count // sub_count)
    slot_count = sub_count * capacity
    owner = parent_of[:, 0]
    order_ids = jnp.arange(child_count, dtype=jnp.int32)
    earlier = (owner[:, None] == owner[None, :]) & (order_ids[None, :] < order_ids[:, None])
    position = jnp.sum(earlier.astype(jnp.int32), axis=1)
    slot_index = owner * capacity + position
    picked = pick_blocks(modes, coupling_pairs)
    row_send = to_slots(row_block, slot_index, slot_count).reshape(sub_count, capacity)
    record = weighted_records(coupling, picked, mode_weights)
    record_send = to_slots(record, slot_index, slot_count).reshape(
        sub_count, capacity, BLK, mode_cols
    )
    record_recv, row_recv = (
        lax.all_to_all(record_send, "sub", split_axis=0, concat_axis=0, tiled=True),
        lax.all_to_all(row_send, "sub", split_axis=0, concat_axis=0, tiled=True),
    )
    records = record_recv.reshape(slot_count, BLK, mode_cols)
    row_index = row_recv.reshape(slot_count)
    sep_blocks = parent_modes.shape[1] // BLK
    parent_blocks = parent_modes[0].reshape(sep_blocks, BLK, MP)
    group_size = min(64, slot_count)
    group_count = slot_count // group_size
    record_groups = records.reshape(group_count, group_size, BLK, mode_cols)
    row_groups = row_index.reshape(group_count, group_size)

    def project(gram_sum, members):
        record_part, row_part = members
        selector = (row_part[:, None] == jnp.arange(sep_blocks, dtype=jnp.int32)[None, :]).astype(
            jnp.bfloat16
        )
        parent_rows = jnp.einsum(
            "sb,bik->sik", selector, parent_blocks, preferred_element_type=jnp.float32
        ).astype(jnp.bfloat16)
        projected = jnp.einsum(
            "sik,sim->skm", parent_rows, record_part, preferred_element_type=jnp.float32
        ).astype(jnp.bfloat16)
        term = jnp.einsum("skm,slm->kl", projected, projected, preferred_element_type=jnp.float32)
        return (gram_sum + term, projected)

    gram_sum, projected_all = lax.scan(
        project, jnp.zeros((MP, MP), jnp.float32), (record_groups, row_groups)
    )
    gram_sum = lax.psum(gram_sum, "mode")
    pencil = jnp.diag(parent_eigs[0]) + gram_sum / (CH_DEV * M)
    factor = jnp.linalg.cholesky(pencil)
    identity = jnp.eye(MP, dtype=pencil.dtype)
    inverse = lax.linalg.triangular_solve(factor, identity, left_side=True, lower=True).astype(
        jnp.bfloat16
    )

    def strength(projected):
        rotated = jnp.einsum("kl,slm->skm", inverse, projected, preferred_element_type=jnp.float32)
        return jnp.sum(rotated * rotated, axis=1) / MP

    slot_values = lax.map(strength, projected_all).reshape(sub_count, capacity, mode_cols)
    returned = lax.all_to_all(slot_values, "sub", split_axis=0, concat_axis=0, tiled=True)
    return returned.reshape(slot_count, mode_cols)[slot_index]


def solution(mesh):
    in_specs = (
        P("sub", None, None),
        P("sub", None),
        P("sub", None, "mode"),
        P("sub", "mode"),
        P("sub", None),
        P("sub"),
        P("sub", None, None),
        P("sub", None),
    )
    out_specs = P("sub", "mode")
    return jax.shard_map(
        per_device, mesh=mesh, in_specs=in_specs, out_specs=out_specs, check_vma=False
    )
```

profile of v0, /device:TPU:0, one launch (start us, length us, event | category | flops | bytes accessed | tf_op | source)
XLA Modules:
  0.0 229.0 jit_solution(5430570650498612388)
XLA Ops:
  6.5 0.9 convert_reduce_fusion
  8.1 0.9 scatter_custom_fusion
  9.7 8.3 %all-to-all-start = ((s32[16,1,8]{2,1,0:T(1,128)}), s32[16,1,8]{2,1,0:T(1,128)S(1)}, u32[]{:S(2)}, u32[]{:S(2)}) async-start(s32[16,1,8]{2,1,0:T(1,128)} %bitcast.6), calls=%async_computation | async-start | bytes 16384 | tf_op jit(solution)/shard_map/all_to_all | solution.py:56
  18.9 5.6 %fusion.15 = bf16[64,2,64,128]{3,1,2,0:T(2,128)(2,1)S(1)} fusion(bf16[64,4,64,128]{3,2,1,0:T(8,128)(2,1)} %bitcast.113, s32[64,2]{1,0:T(8,128)S(1)} %copy.57), kind=kOutput, calls=%fused_computation.27 | convolution fusion | flops 9437696 | bytes 6291968 | tf_op jit(solution)/shard_map/skb,sbim->skim/dot_general | solution.py:19
  25.2 1.7 fusion.18
  27.4 6.2 %scatter_fusion = bf16[128,64,128]{2,1,0:T(8,128)(2,1)S(1)} fusion(bf16[128,64,128]{2,1,0:T(8,128)(2,1)S(1)} %broadcast_in_dim.55, s32[64]{0:T(128)S(1)} %fusion.31, bf16[64,64,128]{2,1,0:T(8,128)(2,1)} %fusion.18), kind=kCustom, calls=%fused_computation.2 | custom fusion | bytes 3145984 | tf_op jit(solution)/shard_map/scatter | solution.py:32
  33.6 1.4 copy-done.1
  35.0 6.9 %all-to-all-start.1 = ((bf16[16,8,64,128]{3,2,1,0:T(8,128)(2,1)}), bf16[16,8,64,128]{3,2,1,0:T(8,128)(2,1)S(1)}, u32[]{:S(2)}, u32[]{:S(2)}) async-start(bf16[16,8,64,128]{3,2,1,0:T(8,128)(2,1)} %bitcast.107), calls=%async_computation.1 | async-start | bytes 4194304 | tf_op jit(solution)/shard_map/all_to_all | solution.py:55
  42.0 1.1 copy.60
  44.4 40.2 %all-to-all-done.1 = bf16[16,8,64,128]{3,2,1,0:T(8,128)(2,1)S(1)} async-done(((bf16[16,8,64,128]{3,2,1,0:T(8,128)(2,1)}), bf16[16,8,64,128]{3,2,1,0:T(8,128)(2,1)S(1)}, u32[]{:S(2)}, u32[]{:S(2)}) %all-to-all-start.1) | async-done | bytes 2097184 | tf_op jit(solution)/shard_map/all_to_all | solution.py:55
  84.6 24.0 %while.26 = (s32[]{:T(128)}, f32[256,256]{1,0:T(8,128)}, bf16[2,64,256,128]{3,2,1,0:T(8,128)(2,1)}, s32[2,64]{1,0:T(2,128)S(1)}, bf16[8,64,256]{2,0,1:T(8,128)(2...) while((s32[]{:T(128)}, f32[256,256]{1,0:T(8,128)}, ...), condition=%wide.region_4.5_spmd.clone, body=%wide.region_3.4_spmd.clone.sunk | while | flops 1362231808 | bytes 18614116 | solution.py:81
  85.4 5.7 %bitcast_dynamic-update-slice_fusion.8 = (bf16[2,64,256,128]{3,2,1,0:T(8,128)(2,1)}, bf16[64,256,128]{2,1,0:T(8,128)(2,1)}) fusion(bf16[2,64,256,128]{3,2,1,0:T(8,128)(2,1)} %get-tuple-element.287, s32[]{:T(128)} %get-tuple-element.285, bf16[2,64,64,128]{3,2,1,0:T(8,128)(2,1)S(1)} %get-tuple-element.298, ...), kind=kOutput, calls=%fused_computation.11.clone.1 | convolution fusion | flops 270532608 | bytes 11535360 | tf_op jit(solution)/shard_map/while/body/eval_jaxpr/sik,sim->skm/dot_general | solution.py:75
  91.1 5.5 %fusion.62 = f32[256,256]{1,0:T(8,128)} fusion(bf16[64,256,128]{2,1,0:T(8,128)(2,1)} %get-tuple-element.275, f32[256,256]{1,0:T(8,128)} %get-tuple-element.286, pred[]{:T(512)S(6)} %compare.26), kind=kOutput, calls=%fused_computation.16.clone.1 | convolution fusion | flops 1073872896 | bytes 4718593 | tf_op jit(solution)/shard_map/while/body/eval_jaxpr/skm,slm->kl/dot_general | solution.py:78
  97.3 5.8 %bitcast_dynamic-update-slice_fusion.8 = (bf16[2,64,256,128]{3,2,1,0:T(8,128)(2,1)}, bf16[64,256,128]{2,1,0:T(8,128)(2,1)}) fusion(bf16[2,64,256,128]{3,2,1,0:T(8,128)(2,1)} %get-tuple-element.287, s32[]{:T(128)} %get-tuple-element.285, bf16[2,64,64,128]{3,2,1,0:T(8,128)(2,1)S(1)} %get-tuple-element.298, ...), kind=kOutput, calls=%fused_computation.11.clone.1 | convolution fusion | flops 270532608 | bytes 11535360 | tf_op jit(solution)/shard_map/while/body/eval_jaxpr/sik,sim->skm/dot_general | solution.py:75
  103.1 5.5 %fusion.62 = f32[256,256]{1,0:T(8,128)} fusion(bf16[64,256,128]{2,1,0:T(8,128)(2,1)} %get-tuple-element.275, f32[256,256]{1,0:T(8,128)} %get-tuple-element.286, pred[]{:T(512)S(6)} %compare.26), kind=kOutput, calls=%fused_computation.16.clone.1 | convolution fusion | flops 1073872896 | bytes 4718593 | tf_op jit(solution)/shard_map/while/body/eval_jaxpr/skm,slm->kl/dot_general | solution.py:78
  108.6 1.8 copy.61
  110.5 22.5 %all-reduce.3.cloned.1.call-done = f32[256,256]{0,1:T(8,128)} async-done(((f32[256,256]{0,1:T(8,128)}), f32[256,256]{0,1:T(8,128)}) %all-reduce.3.cloned.1.call-update) | async-done | bytes 262160 | tf_op jit(solution)/shard_map/psum | solution.py:84
  133.0 1.0 multiply_add_fusion
  134.1 1.0 fusion.19
  135.2 11.7 %cholesky.49 = f32[128,128]{1,0:T(8,128)S(1)} custom-call(f32[128,128]{1,0:T(8,128)S(1)} %cholesky.115), custom_call_target="Cholesky" | custom-call | tf_op jit(solution)/shard_map/jit(cholesky)/cholesky | solution.py:86
  146.9 9.8 %custom-call.14 = f32[1,128,128]{1,2,0:T(8,128)S(1)} custom-call(f32[1,128,128]{2,1,0:T(8,128)S(1)} %get-tuple-element.177), custom_call_target="InvertDiagBlocksLowerTriangular" | custom-call | tf_op jit(solution)/shard_map/jit(cholesky)/cholesky | solution.py:86
  157.2 11.7 %cholesky.103 = f32[128,128]{1,0:T(8,128)S(1)} custom-call(f32[128,128]{1,0:T(8,128)S(1)} %convolution_subtract_fusion.1), custom_call_target="Cholesky" | custom-call | tf_op jit(solution)/shard_map/jit(cholesky)/cholesky | solution.py:86
  171.3 4.0 %while.25 = (s32[]{:T(128)}, f32[256,256]{0,1:T(8,128)S(1)}, s32[2,2]{1,0:T(2,128)S(1)}, f32[2,128,128]{2,1,0:T(8,128)S(1)}, s32[]{:T(128)}) while((s32[]{:T(128)}, f32[256,256]{0,1:T(8,128)S(1)}, s32[2,2]{1,0:T(2,128)S(1)}, f32[2,128,128]{2,1,0:T(8,128)S(1)}, s32[]{:T(128)}) %tuple.70), condition=%wide.while_cond, body=%wide.while_body.sunk | while | flops 2 | bytes 393321 | solution.py:88
  171.8 1.3 dynamic-slice.7
  173.8 1.3 dynamic-slice.7
  175.3 19.9 %custom-call.15 = f32[2,128,128]{1,2,0:T(8,128)S(1)} custom-call(f32[2,128,128]{2,1,0:T(8,128)S(1)} %get-tuple-element.70), custom_call_target="InvertDiagBlocksLowerTriangular" | custom-call | tf_op jit(solution)/shard_map/triangular_solve | solution.py:88
  196.2 10.5 %while.24 = (s32[]{:T(128)}, f32[2,64,128]{2,1,0:T(8,128)}, bf16[2,64,256,128]{3,2,1,0:T(8,128)(2,1)}, bf16[256,256]{1,0:T(8,128)(2,1)S(1)}, s32[]{:T(128)}) while((s32[]{:T(128)}, f32[2,64,128]{2,1,0:T(8,128)}, bf16[2,64,256,128]{3,2,1,0:T(8,128)(2,1)}, bf16[256,256]{1,0:T(8,128)(2,1)S(1)}, s32[]{:T(128)}) %tuple.73), condition=%wide.region_12.13_spmd, body=%wide.region_10.12_spmd.sunk | while | flops 1077936128 | bytes 4424765 | solution.py:96
  196.2 4.6 %multiply_reduce_fusion.2 = f32[64,128]{1,0:T(8,128)S(1)} fusion(bf16[2,64,256,128]{3,2,1,0:T(8,128)(2,1)} %get-tuple-element.328, s32[]{:T(128)} %get-tuple-element.321, bf16[256,256]{1,0:T(8,128)(2,1)S(1)} %get-tuple-element.329), kind=kOutput, calls=%fused_computation.3.clone.1 | convolution fusion | flops 1077927936 | bytes 4358656 | tf_op jit(solution)/shard_map/while/body/eval_jaxpr/kl,slm->skm/dot_general | solution.py:93
  201.4 4.6 %multiply_reduce_fusion.2 = f32[64,128]{1,0:T(8,128)S(1)} fusion(bf16[2,64,256,128]{3,2,1,0:T(8,128)(2,1)} %get-tuple-element.328, s32[]{:T(128)} %get-tuple-element.321, bf16[256,256]{1,0:T(8,128)(2,1)S(1)} %get-tuple-element.329), kind=kOutput, calls=%fused_computation.3.clone.1 | convolution fusion | flops 1077927936 | bytes 4358656 | tf_op jit(solution)/shard_map/while/body/eval_jaxpr/kl,slm->skm/dot_general | solution.py:93
  206.6 6.8 %all-to-all-start.2 = ((f32[16,8,128]{2,1,0:T(8,128)}), f32[16,8,128]{2,1,0:T(8,128)S(1)}, u32[]{:S(2)}, u32[]{:S(2)}) async-start(f32[16,8,128]{2,1,0:T(8,128)} %bitcast.21), calls=%async_computation.2 | async-start | bytes 131072 | tf_op jit(solution)/shard_map/all_to_all | solution.py:97
  213.5 7.5 %all-to-all-done.2 = f32[16,8,128]{2,1,0:T(8,128)S(1)} async-done(((f32[16,8,128]{2,1,0:T(8,128)}), f32[16,8,128]{2,1,0:T(8,128)S(1)}, u32[]{:S(2)}, u32[]{:S(2)}) %all-to-all-start.2) | async-done | bytes 65568 | tf_op jit(solution)/shard_map/all_to_all | solution.py:97
  221.0 1.2 gather_fusion
  (59 shorter events, 11.6 us)
Async XLA Ops:
  6.5 18.6 %copy-start = (bf16[64,64,128]{2,1,0:T(8,128)(2,1)S(1)}, bf16[64,64,128]{2,1,0:T(8,128)(2,1)}, u32[]{:S(2)}) copy-start(bf16[64,64,128]{2,1,0:T(8,128)(2,1)} %param.12) | copy-start | bytes 3145732
  9.7 23.8 %all-to-all-start = ((s32[16,1,8]{2,1,0:T(1,128)}), s32[16,1,8]{2,1,0:T(1,128)S(1)}, u32[]{:S(2)}, u32[]{:S(2)}) async-start(s32[16,1,8]{2,1,0:T(1,128)} %bitcast.6), calls=%async_computation | async-start | bytes 16384 | tf_op jit(solution)/shard_map/all_to_all | solution.py:56
  24.5 0.7 copy-start.2
  33.6 1.4 copy-start.1
  35.0 49.6 %all-to-all-start.1 = ((bf16[16,8,64,128]{3,2,1,0:T(8,128)(2,1)}), bf16[16,8,64,128]{3,2,1,0:T(8,128)(2,1)S(1)}, u32[]{:S(2)}, u32[]{:S(2)}) async-start(bf16[16,8,64,128]{3,2,1,0:T(8,128)(2,1)} %bitcast.107), calls=%async_computation.1 | async-start | bytes 4194304 | tf_op jit(solution)/shard_map/all_to_all | solution.py:55
  41.9 91.1 %all-reduce.3.cloned.1.call-start = ((), (), s32[]{:S(2)}) async-start(), calls=%async_computation.3 | async-start | bytes 524288 | tf_op jit(solution)/shard_map/psum | solution.py:84
  84.6 48.4 %copy-start.3 = (f32[1,256]{1,0:T(1,128)S(1)}, f32[1,256]{1,0:T(1,128)}, u32[]{:S(2)}) copy-start(f32[1,256]{1,0:T(1,128)} %param.19) | copy-start | bytes 3076
  206.6 14.4 %all-to-all-start.2 = ((f32[16,8,128]{2,1,0:T(8,128)}), f32[16,8,128]{2,1,0:T(8,128)S(1)}, u32[]{:S(2)}, u32[]{:S(2)}) async-start(f32[16,8,128]{2,1,0:T(8,128)} %bitcast.21), calls=%async_computation.2 | async-start | bytes 131072 | tf_op jit(solution)/shard_map/all_to_all | solution.py:97
Sparse Core Ops, SparseCore 0:
  110.5 22.4 all-reduce.2
where the time goes:
time: 230 us; the launch traced here: 229 us
  waiting for transfers between devices  70.3 us (31%)
  other arithmetic  59.4 us (26%)
  matrix products  41.9 us (18%)
  starting transfers between devices  22.1 us (10%)
  local copies, waits for them, and re-layouts  20.3 us (9%)
  between operations  14.9 us (6%)
    all_to_all x1, waiting for transfers between devices, per_device(): lax.all_to_all(record_send, 'sub', split_axis=0, concat_axis=0, tiled=True)  40.2 us
    another operation x6, other arithmetic, per_device(): factor = jnp.linalg.cholesky(pencil)  34 us
    psum x1, waiting for transfers between devices, per_device(): gram_sum = lax.psum(gram_sum, 'mode')  22.5 us
    another operation x4, other arithmetic, per_device(): lax.linalg.triangular_solve(factor, identity, left_side=True, lower=True)  19.9 us
    dot_general x2, matrix products, project(): jnp.einsum('sik,sim->skm', parent_rows, record_part, preferred_element_ty...  11.5 us
    dot_general x2, matrix products, project(): jnp.einsum('skm,slm->kl', projected, projected, preferred_element_type=jn...  11 us
    dot_general x2, matrix products, strength(): jnp.einsum('kl,slm->skm', inverse, projected, preferred_element_type=jnp....  9.22 us
    all_to_all x1, starting transfers between devices, per_device(): lax.all_to_all(row_send, 'sub', split_axis=0, concat_axis=0, tiled=True)  8.34 us
  transfers between devices with their start and end apart: 4, of which 3 were waited for; matrix products, arithmetic and copies ran while one was open for 8% of the time, Pallas kernels for 0%

commit v1 on v0

--- a/solution.py
+++ b/solution.py
@@ -7,6 +7,29 @@
 MP = 256
 BLK = 64
 CH_DEV = 64
+
+
+def cut_along(value, dim, devices):
+    shape = value.shape
+    blocks = value.reshape(*shape[:dim], devices, shape[dim] // devices, *shape[dim + 1 :])
+    return jnp.moveaxis(blocks, dim, 0)
+
+
+def in_order(parts, dim):
+    dims = list(parts.shape[1:])
+    dims[dim] *= parts.shape[0]
+    return jnp.moveaxis(parts, 0, dim).reshape(dims)
+
+
+def sent_to_each(value, axis, split_dim, concat_dim):
+    size, position = (lax.axis_size(axis), lax.axis_index(axis))
+    blocks = cut_along(value, split_dim, size)
+    finished = [blocks[position]]
+    for turn in range(1, size):
+        sent = blocks[(position + turn) % size]
+        finished.append(lax.ppermute(sent, axis, [(i, (i + turn) % size) for i in range(size)]))
+    blocks = jnp.stack(finished)[(position - jnp.arange(size)) % size]
+    return in_order(blocks, concat_dim)
 
 
 def pick_blocks(modes, coupling_pairs):
@@ -52,7 +75,7 @@
         sub_count, capacity, BLK, mode_cols
     )
     record_recv, row_recv = (
-        lax.all_to_all(record_send, "sub", split_axis=0, concat_axis=0, tiled=True),
+        sent_to_each(record_send, "sub", 0, 0),
         lax.all_to_all(row_send, "sub", split_axis=0, concat_axis=0, tiled=True),
     )
     records = record_recv.reshape(slot_count, BLK, mode_cols)

time: 230 us -> 241 us (1.048)
  waiting for transfers between devices: 70.3 us -> 49.1 us
  starting transfers between devices: 22.1 us -> 42.8 us
  local copies, waits for them, and re-layouts: 20.3 us -> 32.2 us
    all_to_all x1 -> x0, waiting for transfers between devices: 40.2 us -> none  [per_device(): lax.all_to_all(record_send, 'sub', split_axis=0, concat_axis=0, tiled=True)]
    ppermute x0 -> x15, starting transfers between devices: none -> 30.4 us  [sent_to_each(): lax.ppermute(sent, axis, [(i, (i + turn) % size) for i in range(size)])]
    ppermute x0 -> x15, waiting for transfers between devices: none -> 10.6 us  [sent_to_each(): lax.ppermute(sent, axis, [(i, (i + turn) % size) for i in range(size)])]
    all_to_all x1, waiting for transfers between devices: 0.01 us -> 7.46 us  [per_device(): lax.all_to_all(row_send, 'sub', split_axis=0, concat_axis=0, tiled=True)]
    unnamed x10 -> x30, local copies, waits for them, and re-layouts: 3.39 us -> 10.3 us
    all_to_all x1 -> x0, starting transfers between devices: 6.91 us -> none  [per_device(): lax.all_to_all(record_send, 'sub', split_axis=0, concat_axis=0, tiled=True)]
    all_to_all x1, starting transfers between devices: 8.34 us -> 5.51 us  [per_device(): lax.all_to_all(row_send, 'sub', split_axis=0, concat_axis=0, tiled=True)]
    gather x0 -> x1, local copies, waits for them, and re-layouts: none -> 2.54 us  [sent_to_each(): blocks = jnp.stack(finished)[(position - jnp.arange(size)) % size]]
  transfers between devices with their start and end apart: 4 -> 18, of which waited for: 3 -> 6; matrix products, arithmetic and copies ran while one was open for 8% -> 5% of each run, Pallas kernels for 0% -> 0%
where the time goes in v1:
time: 241 us; the launch traced here: 240 us
  other arithmetic  59.5 us (25%)
  waiting for transfers between devices  49.1 us (20%)
  starting transfers between devices  42.8 us (18%)
  matrix products  41.8 us (17%)
  local copies, waits for them, and re-layouts  32.2 us (13%)
  between operations  14.9 us (6%)
    another operation x6, other arithmetic, per_device(): factor = jnp.linalg.cholesky(pencil)  34 us
    ppermute x15, starting transfers between devices, sent_to_each(): lax.ppermute(sent, axis, [(i, (i + turn) % size) for i in range(size)])  30.4 us
    psum x1, waiting for transfers between devices, per_device(): gram_sum = lax.psum(gram_sum, 'mode')  23.5 us
    another operation x4, other arithmetic, per_device(): lax.linalg.triangular_solve(factor, identity, left_side=True, lower=True)  19.9 us
    dot_general x2, matrix products, project(): jnp.einsum('sik,sim->skm', parent_rows, record_part, preferred_element_ty...  11.5 us
    dot_general x2, matrix products, project(): jnp.einsum('skm,slm->kl', projected, projected, preferred_element_type=jn...  10.9 us
    ppermute x15, waiting for transfers between devices, sent_to_each(): lax.ppermute(sent, axis, [(i, (i + turn) % size) for i in range(size)])  10.6 us
    unnamed x30, local copies, waits for them, and re-layouts  10.3 us
  transfers between devices with their start and end apart: 18, of which 6 were waited for; matrix products, arithmetic and copies ran while one was open for 5% of the time, Pallas kernels for 0%

profile of v1, /device:TPU:0, one launch (start us, length us, event | category | flops | bytes accessed | tf_op | source)
XLA Modules:
  0.0 240.4 jit_solution(16793259946870694766)
XLA Ops:
  8.9 5.6 %fusion.15 = bf16[64,2,64,128]{3,1,2,0:T(2,128)(2,1)S(1)} fusion(bf16[64,4,64,128]{3,2,1,0:T(8,128)(2,1)} %bitcast.177, s32[64,2]{1,0:T(8,128)S(1)} %copy.57), kind=kOutput, calls=%fused_computation.28 | convolution fusion | flops 9437696 | bytes 6291968 | tf_op jit(solution)/shard_map/skb,sbim->skim/dot_general | solution.py:42
  17.4 6.2 %scatter_fusion = bf16[128,64,128]{2,1,0:T(8,128)(2,1)S(1)} fusion(bf16[128,64,128]{2,1,0:T(8,128)(2,1)S(1)} %broadcast_in_dim.56, s32[64]{0:T(128)S(1)} %fusion.32, bf16[64,64,128]{2,1,0:T(8,128)(2,1)} %fusion.18), kind=kCustom, calls=%fused_computation.3 | custom fusion | bytes 3145984 | tf_op jit(solution)/shard_map/scatter | solution.py:55
  25.2 3.0 %collective-permute-start = (bf16[1,8,64,128]{3,2,1,0:T(8,128)(2,1)}, bf16[1,8,64,128]{3,2,1,0:T(8,128)(2,1)S(1)}, u32[]{:S(2)}, u32[]{:S(2)}) collective-permute-start(bf16[1,8,64,128]{3,2,1,0:T(8,128)(2,1)} %get-tuple-element.190), channel_id=1, source_target_pairs={{0,2},{2,4},{4,6},{6,8},{8,10},{10,12},{12,14},{14,16},{16,18},{18... | collective-permute-start | bytes 393224 | tf_op jit(solution)/shard_map/ppermute | solution.py:30
  29.7 2.4 %collective-permute-start.2 = (bf16[1,8,64,128]{3,2,1,0:T(8,128)(2,1)}, bf16[1,8,64,128]{3,2,1,0:T(8,128)(2,1)S(1)}, u32[]{:S(2)}, u32[]{:S(2)}) collective-permute-start(bf16[1,8,64,128]{3,2,1,0:T(8,128)(2,1)} %get-tuple-element.188), channel_id=1, source_target_pairs={{0,6},{2,8},{4,10},{6,12},{8,14},{10,16},{12,18},{14,20},{16,22},{... | collective-permute-start | bytes 393224 | tf_op jit(solution)/shard_map/ppermute | solution.py:30
  37.0 5.5 %all-to-all-start = ((s32[16,1,8]{2,1,0:T(1,128)}), s32[16,1,8]{2,1,0:T(1,128)S(1)}, u32[]{:S(2)}, u32[]{:S(2)}) async-start(s32[16,1,8]{2,1,0:T(1,128)} %bitcast.6), calls=%async_computation | async-start | bytes 16384 | tf_op jit(solution)/shard_map/all_to_all | solution.py:79
  42.7 7.5 %all-to-all-done = s32[16,1,8]{2,1,0:T(1,128)S(1)} async-done(((s32[16,1,8]{2,1,0:T(1,128)}), s32[16,1,8]{2,1,0:T(1,128)S(1)}, u32[]{:S(2)}, u32[]{:S(2)}) %all-to-all-start) | async-done | bytes 544 | tf_op jit(solution)/shard_map/all_to_all | solution.py:79
  52.7 2.4 %collective-permute-start.6 = (bf16[1,8,64,128]{3,2,1,0:T(8,128)(2,1)}, bf16[1,8,64,128]{3,2,1,0:T(8,128)(2,1)S(1)}, u32[]{:S(2)}, u32[]{:S(2)}) collective-permute-start(bf16[1,8,64,128]{3,2,1,0:T(8,128)(2,1)} %get-tuple-element.184), channel_id=1, source_target_pairs={{0,14},{2,16},{4,18},{6,20},{8,22},{10,24},{12,26},{14,28},{16,30}... | collective-permute-start | bytes 393224 | tf_op jit(solution)/shard_map/ppermute | solution.py:30
  60.0 2.3 collective-permute-start.9
  63.0 6.9 %collective-permute-done.5 = bf16[1,8,64,128]{3,2,1,0:T(8,128)(2,1)S(1)} collective-permute-done((bf16[1,8,64,128]{3,2,1,0:T(8,128)(2,1)}, bf16[1,8,64,128]{3,2,1,0:T(8,128)(2,1)S(1)}, u32[]{:S(2)}, u32[]{:S(2)}) %collective-permute-start.5) | collective-permute-done | bytes 131104 | tf_op jit(solution)/shard_map/ppermute | solution.py:30
  70.6 2.1 collective-permute-done.6
  72.7 4.5 %collective-permute-start.11 = (bf16[1,8,64,128]{3,2,1,0:T(8,128)(2,1)S(1)}, bf16[1,8,64,128]{3,2,1,0:T(8,128)(2,1)S(1)}, u32[]{:S(2)}, u32[]{:S(2)}) collective-permute-start(bf16[1,8,64,128]{3,2,1,0:T(8,128)(2,1)S(1)} %copy-done.4), channel_id=1, source_target_pairs={{0,24},{2,26},{4,28},{6,30},{8,0},{10,2},{12,4},{14,6},{16,8},{18,... | collective-permute-start | bytes 393224 | tf_op jit(solution)/shard_map/ppermute | solution.py:30
  77.8 3.1 %collective-permute-start.12 = (bf16[1,8,64,128]{3,2,1,0:T(8,128)(2,1)S(1)}, bf16[1,8,64,128]{3,2,1,0:T(8,128)(2,1)S(1)}, u32[]{:S(2)}, u32[]{:S(2)}) collective-permute-start(bf16[1,8,64,128]{3,2,1,0:T(8,128)(2,1)S(1)} %copy-done.3), channel_id=1, source_target_pairs={{0,26},{2,28},{4,30},{6,0},{8,2},{10,4},{12,6},{14,8},{16,10},{18,... | collective-permute-start | bytes 393224 | tf_op jit(solution)/shard_map/ppermute | solution.py:30
  81.6 2.3 collective-permute-start.13
  84.6 2.0 collective-permute-start.14
  92.3 2.5 %gather_fusion = bf16[16,8,64,128]{3,2,1,0:T(8,128)(2,1)S(1)} fusion(bf16[16,8,64,128]{3,2,1,0:T(8,128)(2,1)} %bitcast.172, s32[1024]{0:T(1024)S(1)} %pad_clamp_fusion.1), kind=kCustom, calls=%fused_computation | custom fusion | bytes 4194368 | tf_op jit(solution)/shard_map/gather | solution.py:31
  94.8 24.0 %while.26 = (s32[]{:T(128)}, f32[256,256]{1,0:T(8,128)}, bf16[2,64,256,128]{3,2,1,0:T(8,128)(2,1)}, s32[2,64]{1,0:T(2,128)S(1)}, bf16[8,64,256]{2,0,1:T(8,128)(2...) while((s32[]{:T(128)}, f32[256,256]{1,0:T(8,128)}, ...), condition=%wide.region_4.5_spmd.clone, body=%wide.region_3.4_spmd.clone.sunk | while | flops 1362231808 | bytes 18614116 | solution.py:104
  95.6 5.7 %bitcast_dynamic-update-slice_fusion.23 = (bf16[2,64,256,128]{3,2,1,0:T(8,128)(2,1)}, bf16[64,256,128]{2,1,0:T(8,128)(2,1)}) fusion(bf16[2,64,256,128]{3,2,1,0:T(8,128)(2,1)} %get-tuple-element.303, s32[]{:T(128)} %get-tuple-element.301, bf16[2,64,64,128]{3,2,1,0:T(8,128)(2,1)S(1)} %get-tuple-element.314, ...), kind=kOutput, calls=%fused_computation.12.clone.1 | convolution fusion | flops 270532608 | bytes 11535360 | tf_op jit(solution)/shard_map/while/body/eval_jaxpr/sik,sim->skm/dot_general | solution.py:98
  101.3 5.4 %fusion.64 = f32[256,256]{1,0:T(8,128)} fusion(bf16[64,256,128]{2,1,0:T(8,128)(2,1)} %get-tuple-element.291, f32[256,256]{1,0:T(8,128)} %get-tuple-element.302, pred[]{:T(512)S(6)} %compare.48), kind=kOutput, calls=%fused_computation.17.clone.1 | convolution fusion | flops 1073872896 | bytes 4718593 | tf_op jit(solution)/shard_map/while/body/eval_jaxpr/skm,slm->kl/dot_general | solution.py:101
  107.5 5.8 %bitcast_dynamic-update-slice_fusion.23 = (bf16[2,64,256,128]{3,2,1,0:T(8,128)(2,1)}, bf16[64,256,128]{2,1,0:T(8,128)(2,1)}) fusion(bf16[2,64,256,128]{3,2,1,0:T(8,128)(2,1)} %get-tuple-element.303, s32[]{:T(128)} %get-tuple-element.301, bf16[2,64,64,128]{3,2,1,0:T(8,128)(2,1)S(1)} %get-tuple-element.314, ...), kind=kOutput, calls=%fused_computation.12.clone.1 | convolution fusion | flops 270532608 | bytes 11535360 | tf_op jit(solution)/shard_map/while/body/eval_jaxpr/sik,sim->skm/dot_general | solution.py:98
  113.4 5.4 %fusion.64 = f32[256,256]{1,0:T(8,128)} fusion(bf16[64,256,128]{2,1,0:T(8,128)(2,1)} %get-tuple-element.291, f32[256,256]{1,0:T(8,128)} %get-tuple-element.302, pred[]{:T(512)S(6)} %compare.48), kind=kOutput, calls=%fused_computation.17.clone.1 | convolution fusion | flops 1073872896 | bytes 4718593 | tf_op jit(solution)/shard_map/while/body/eval_jaxpr/skm,slm->kl/dot_general | solution.py:101
  118.8 1.8 copy.61
  120.7 23.5 %all-reduce.3.cloned.1.call-done = f32[256,256]{0,1:T(8,128)} async-done(((f32[256,256]{0,1:T(8,128)}), f32[256,256]{0,1:T(8,128)}) %all-reduce.3.cloned.1.call-update) | async-done | bytes 262160 | tf_op jit(solution)/shard_map/psum | solution.py:107
  146.3 11.7 %cholesky.49 = f32[128,128]{1,0:T(8,128)S(1)} custom-call(f32[128,128]{1,0:T(8,128)S(1)} %cholesky.115), custom_call_target="Cholesky" | custom-call | tf_op jit(solution)/shard_map/jit(cholesky)/cholesky | solution.py:109
  158.1 9.8 %custom-call.14 = f32[1,128,128]{1,2,0:T(8,128)S(1)} custom-call(f32[1,128,128]{2,1,0:T(8,128)S(1)} %get-tuple-element.193), custom_call_target="InvertDiagBlocksLowerTriangular" | custom-call | tf_op jit(solution)/shard_map/jit(cholesky)/cholesky | solution.py:109
  168.4 11.7 %cholesky.103 = f32[128,128]{1,0:T(8,128)S(1)} custom-call(f32[128,128]{1,0:T(8,128)S(1)} %convolution_subtract_fusion.1), custom_call_target="Cholesky" | custom-call | tf_op jit(solution)/shard_map/jit(cholesky)/cholesky | solution.py:109
  182.5 4.1 %while.25 = (s32[]{:T(128)}, f32[256,256]{0,1:T(8,128)S(1)}, s32[2,2]{1,0:T(2,128)S(1)}, f32[2,128,128]{2,1,0:T(8,128)S(1)}, s32[]{:T(128)}) while((s32[]{:T(128)}, f32[256,256]{0,1:T(8,128)S(1)}, s32[2,2]{1,0:T(2,128)S(1)}, f32[2,128,128]{2,1,0:T(8,128)S(1)}, s32[]{:T(128)}) %tuple.85), condition=%wide.while_cond, body=%wide.while_body.sunk | while | flops 2 | bytes 393321 | solution.py:111
  186.6 19.9 %custom-call.15 = f32[2,128,128]{1,2,0:T(8,128)S(1)} custom-call(f32[2,128,128]{2,1,0:T(8,128)S(1)} %get-tuple-element.70), custom_call_target="InvertDiagBlocksLowerTriangular" | custom-call | tf_op jit(solution)/shard_map/triangular_solve | solution.py:111
  207.5 10.5 %while.24 = (s32[]{:T(128)}, f32[2,64,128]{2,1,0:T(8,128)}, bf16[2,64,256,128]{3,2,1,0:T(8,128)(2,1)}, bf16[256,256]{1,0:T(8,128)(2,1)S(1)}, s32[]{:T(128)}) while((s32[]{:T(128)}, f32[2,64,128]{2,1,0:T(8,128)}, bf16[2,64,256,128]{3,2,1,0:T(8,128)(2,1)}, bf16[256,256]{1,0:T(8,128)(2,1)S(1)}, s32[]{:T(128)}) %tuple.88), condition=%wide.region_12.13_spmd, body=%wide.region_10.12_spmd.sunk | while | flops 1077936128 | bytes 4424765 | solution.py:119
  207.5 4.6 %multiply_reduce_fusion.2 = f32[64,128]{1,0:T(8,128)S(1)} fusion(bf16[2,64,256,128]{3,2,1,0:T(8,128)(2,1)} %get-tuple-element.344, s32[]{:T(128)} %get-tuple-element.337, bf16[256,256]{1,0:T(8,128)(2,1)S(1)} %get-tuple-element.345), kind=kOutput, calls=%fused_computation.4.clone.1 | convolution fusion | flops 1077927936 | bytes 4358656 | tf_op jit(solution)/shard_map/while/body/eval_jaxpr/kl,slm->skm/dot_general | solution.py:116
  212.8 4.6 %multiply_reduce_fusion.2 = f32[64,128]{1,0:T(8,128)S(1)} fusion(bf16[2,64,256,128]{3,2,1,0:T(8,128)(2,1)} %get-tuple-element.344, s32[]{:T(128)} %get-tuple-element.337, bf16[256,256]{1,0:T(8,128)(2,1)S(1)} %get-tuple-element.345), kind=kOutput, calls=%fused_computation.4.clone.1 | convolution fusion | flops 1077927936 | bytes 4358656 | tf_op jit(solution)/shard_map/while/body/eval_jaxpr/kl,slm->skm/dot_general | solution.py:116
  218.0 6.8 %all-to-all-start.1 = ((f32[16,8,128]{2,1,0:T(8,128)}), f32[16,8,128]{2,1,0:T(8,128)S(1)}, u32[]{:S(2)}, u32[]{:S(2)}) async-start(f32[16,8,128]{2,1,0:T(8,128)} %bitcast.53), calls=%async_computation.1 | async-start | bytes 131072 | tf_op jit(solution)/shard_map/all_to_all | solution.py:120
  224.9 7.5 %all-to-all-done.1 = f32[16,8,128]{2,1,0:T(8,128)S(1)} async-done(((f32[16,8,128]{2,1,0:T(8,128)}), f32[16,8,128]{2,1,0:T(8,128)S(1)}, u32[]{:S(2)}, u32[]{:S(2)}) %all-to-all-start.1) | async-done | bytes 65568 | tf_op jit(solution)/shard_map/all_to_all | solution.py:120
  (112 shorter events, 42.5 us)
Async XLA Ops:
  6.5 8.7 %copy-start = (bf16[64,64,128]{2,1,0:T(8,128)(2,1)S(1)}, bf16[64,64,128]{2,1,0:T(8,128)(2,1)}, u32[]{:S(2)}) copy-start(bf16[64,64,128]{2,1,0:T(8,128)(2,1)} %param.12) | copy-start | bytes 3145732
  14.5 0.7 copy-start.5
  23.6 19.0 %copy-start.1 = (bf16[1,512,256]{2,1,0:T(8,128)(2,1)S(1)}, bf16[1,512,256]{2,1,0:T(8,128)(2,1)}, u32[]{:S(2)}) copy-start(bf16[1,512,256]{2,1,0:T(8,128)(2,1)} %param.18) | copy-start | bytes 786436
  25.2 47.5 %copy-start.4 = (bf16[1,8,64,128]{3,2,1,0:T(8,128)(2,1)S(1)}, bf16[1,8,64,128]{3,2,1,0:T(8,128)(2,1)}, u32[]{:S(2)}) copy-start(bf16[1,8,64,128]{3,2,1,0:T(8,128)(2,1)} %get-tuple-element.179) | copy-start | bytes 393220
  25.2 52.7 %copy-start.3 = (bf16[1,8,64,128]{3,2,1,0:T(8,128)(2,1)S(1)}, bf16[1,8,64,128]{3,2,1,0:T(8,128)(2,1)}, u32[]{:S(2)}) copy-start(bf16[1,8,64,128]{3,2,1,0:T(8,128)(2,1)} %get-tuple-element.178) | copy-start | bytes 393220
  25.2 56.4 %copy-start.2 = (bf16[1,8,64,128]{3,2,1,0:T(8,128)(2,1)S(1)}, bf16[1,8,64,128]{3,2,1,0:T(8,128)(2,1)}, u32[]{:S(2)}) copy-start(bf16[1,8,64,128]{3,2,1,0:T(8,128)(2,1)} %get-tuple-element.177) | copy-start | bytes 393220
  25.2 26.3 %collective-permute-start = (bf16[1,8,64,128]{3,2,1,0:T(8,128)(2,1)}, bf16[1,8,64,128]{3,2,1,0:T(8,128)(2,1)S(1)}, u32[]{:S(2)}, u32[]{:S(2)}) collective-permute-start(bf16[1,8,64,128]{3,2,1,0:T(8,128)(2,1)} %get-tuple-element.190), channel_id=1, source_target_pairs={{0,2},{2,4},{4,6},{6,8},{8,10},{10,12},{12,14},{14,16},{16,18},{18... | collective-permute-start | bytes 393224 | tf_op jit(solution)/shard_map/ppermute | solution.py:30
  28.2 24.5 %collective-permute-start.1 = (bf16[1,8,64,128]{3,2,1,0:T(8,128)(2,1)}, bf16[1,8,64,128]{3,2,1,0:T(8,128)(2,1)S(1)}, u32[]{:S(2)}, u32[]{:S(2)}) collective-permute-start(bf16[1,8,64,128]{3,2,1,0:T(8,128)(2,1)} %get-tuple-element.189), channel_id=1, source_target_pairs={{0,4},{2,6},{4,8},{6,10},{8,12},{10,14},{12,16},{14,18},{16,20},{1... | collective-permute-start | bytes 393224 | tf_op jit(solution)/shard_map/ppermute | solution.py:30
  29.7 26.0 %collective-permute-start.2 = (bf16[1,8,64,128]{3,2,1,0:T(8,128)(2,1)}, bf16[1,8,64,128]{3,2,1,0:T(8,128)(2,1)S(1)}, u32[]{:S(2)}, u32[]{:S(2)}) collective-permute-start(bf16[1,8,64,128]{3,2,1,0:T(8,128)(2,1)} %get-tuple-element.188), channel_id=1, source_target_pairs={{0,6},{2,8},{4,10},{6,12},{8,14},{10,16},{12,18},{14,20},{16,22},{... | collective-permute-start | bytes 393224 | tf_op jit(solution)/shard_map/ppermute | solution.py:30
  32.2 25.6 %collective-permute-start.3 = (bf16[1,8,64,128]{3,2,1,0:T(8,128)(2,1)}, bf16[1,8,64,128]{3,2,1,0:T(8,128)(2,1)S(1)}, u32[]{:S(2)}, u32[]{:S(2)}) collective-permute-start(bf16[1,8,64,128]{3,2,1,0:T(8,128)(2,1)} %get-tuple-element.187), channel_id=1, source_target_pairs={{0,8},{2,10},{4,12},{6,14},{8,16},{10,18},{12,20},{14,22},{16,24},... | collective-permute-start | bytes 393224 | tf_op jit(solution)/shard_map/ppermute | solution.py:30
  33.8 26.3 %collective-permute-start.4 = (bf16[1,8,64,128]{3,2,1,0:T(8,128)(2,1)}, bf16[1,8,64,128]{3,2,1,0:T(8,128)(2,1)S(1)}, u32[]{:S(2)}, u32[]{:S(2)}) collective-permute-start(bf16[1,8,64,128]{3,2,1,0:T(8,128)(2,1)} %get-tuple-element.186), channel_id=1, source_target_pairs={{0,10},{2,12},{4,14},{6,16},{8,18},{10,20},{12,22},{14,24},{16,26}... | collective-permute-start | bytes 393224 | tf_op jit(solution)/shard_map/ppermute | solution.py:30
  37.0 13.2 %all-to-all-start = ((s32[16,1,8]{2,1,0:T(1,128)}), s32[16,1,8]{2,1,0:T(1,128)S(1)}, u32[]{:S(2)}, u32[]{:S(2)}) async-start(s32[16,1,8]{2,1,0:T(1,128)} %bitcast.6), calls=%async_computation | async-start | bytes 16384 | tf_op jit(solution)/shard_map/all_to_all | solution.py:79
  42.5 101.7 %all-reduce.3.cloned.1.call-start = ((), (), s32[]{:S(2)}) async-start(), calls=%async_computation.2 | async-start | bytes 524288 | tf_op jit(solution)/shard_map/psum | solution.py:107
  51.5 18.4 %collective-permute-start.5 = (bf16[1,8,64,128]{3,2,1,0:T(8,128)(2,1)}, bf16[1,8,64,128]{3,2,1,0:T(8,128)(2,1)S(1)}, u32[]{:S(2)}, u32[]{:S(2)}) collective-permute-start(bf16[1,8,64,128]{3,2,1,0:T(8,128)(2,1)} %get-tuple-element.185), channel_id=1, source_target_pairs={{0,12},{2,14},{4,16},{6,18},{8,20},{10,22},{12,24},{14,26},{16,28}... | collective-permute-start | bytes 393224 | tf_op jit(solution)/shard_map/ppermute | solution.py:30
  52.7 20.0 %collective-permute-start.6 = (bf16[1,8,64,128]{3,2,1,0:T(8,128)(2,1)}, bf16[1,8,64,128]{3,2,1,0:T(8,128)(2,1)S(1)}, u32[]{:S(2)}, u32[]{:S(2)}) collective-permute-start(bf16[1,8,64,128]{3,2,1,0:T(8,128)(2,1)} %get-tuple-element.184), channel_id=1, source_target_pairs={{0,14},{2,16},{4,18},{6,20},{8,22},{10,24},{12,26},{14,28},{16,30}... | collective-permute-start | bytes 393224 | tf_op jit(solution)/shard_map/ppermute | solution.py:30
  55.8 22.1 %collective-permute-start.7 = (bf16[1,8,64,128]{3,2,1,0:T(8,128)(2,1)}, bf16[1,8,64,128]{3,2,1,0:T(8,128)(2,1)S(1)}, u32[]{:S(2)}, u32[]{:S(2)}) collective-permute-start(bf16[1,8,64,128]{3,2,1,0:T(8,128)(2,1)} %get-tuple-element.183), channel_id=1, source_target_pairs={{0,16},{2,18},{4,20},{6,22},{8,24},{10,26},{12,28},{14,30},{16,0},... | collective-permute-start | bytes 393224 | tf_op jit(solution)/shard_map/ppermute | solution.py:30
  57.8 23.8 %collective-permute-start.8 = (bf16[1,8,64,128]{3,2,1,0:T(8,128)(2,1)}, bf16[1,8,64,128]{3,2,1,0:T(8,128)(2,1)S(1)}, u32[]{:S(2)}, u32[]{:S(2)}) collective-permute-start(bf16[1,8,64,128]{3,2,1,0:T(8,128)(2,1)} %get-tuple-element.182), channel_id=1, source_target_pairs={{0,18},{2,20},{4,22},{6,24},{8,26},{10,28},{12,30},{14,0},{16,2},{... | collective-permute-start | bytes 393224 | tf_op jit(solution)/shard_map/ppermute | solution.py:30
  60.0 24.6 %collective-permute-start.9 = (bf16[1,8,64,128]{3,2,1,0:T(8,128)(2,1)}, bf16[1,8,64,128]{3,2,1,0:T(8,128)(2,1)S(1)}, u32[]{:S(2)}, u32[]{:S(2)}) collective-permute-start(bf16[1,8,64,128]{3,2,1,0:T(8,128)(2,1)} %get-tuple-element.181), channel_id=1, source_target_pairs={{0,20},{2,22},{4,24},{6,26},{8,28},{10,30},{12,0},{14,2},{16,4},{1... | collective-permute-start | bytes 393224 | tf_op jit(solution)/shard_map/ppermute | solution.py:30
  69.9 17.4 %collective-permute-start.10 = (bf16[1,8,64,128]{3,2,1,0:T(8,128)(2,1)}, bf16[1,8,64,128]{3,2,1,0:T(8,128)(2,1)S(1)}, u32[]{:S(2)}, u32[]{:S(2)}) collective-permute-start(bf16[1,8,64,128]{3,2,1,0:T(8,128)(2,1)} %get-tuple-element.180), channel_id=1, source_target_pairs={{0,22},{2,24},{4,26},{6,28},{8,30},{10,0},{12,2},{14,4},{16,6},{18... | collective-permute-start | bytes 393224 | tf_op jit(solution)/shard_map/ppermute | solution.py:30
  72.7 15.3 %collective-permute-start.11 = (bf16[1,8,64,128]{3,2,1,0:T(8,128)(2,1)S(1)}, bf16[1,8,64,128]{3,2,1,0:T(8,128)(2,1)S(1)}, u32[]{:S(2)}, u32[]{:S(2)}) collective-permute-start(bf16[1,8,64,128]{3,2,1,0:T(8,128)(2,1)S(1)} %copy-done.4), channel_id=1, source_target_pairs={{0,24},{2,26},{4,28},{6,30},{8,0},{10,2},{12,4},{14,6},{16,8},{18,... | collective-permute-start | bytes 393224 | tf_op jit(solution)/shard_map/ppermute | solution.py:30
  77.8 10.8 %collective-permute-start.12 = (bf16[1,8,64,128]{3,2,1,0:T(8,128)(2,1)S(1)}, bf16[1,8,64,128]{3,2,1,0:T(8,128)(2,1)S(1)}, u32[]{:S(2)}, u32[]{:S(2)}) collective-permute-start(bf16[1,8,64,128]{3,2,1,0:T(8,128)(2,1)S(1)} %copy-done.3), channel_id=1, source_target_pairs={{0,26},{2,28},{4,30},{6,0},{8,2},{10,4},{12,6},{14,8},{16,10},{18,... | collective-permute-start | bytes 393224 | tf_op jit(solution)/shard_map/ppermute | solution.py:30
  81.6 7.7 %collective-permute-start.13 = (bf16[1,8,64,128]{3,2,1,0:T(8,128)(2,1)S(1)}, bf16[1,8,64,128]{3,2,1,0:T(8,128)(2,1)S(1)}, u32[]{:S(2)}, u32[]{:S(2)}) collective-permute-start(bf16[1,8,64,128]{3,2,1,0:T(8,128)(2,1)S(1)} %copy-done.2), channel_id=1, source_target_pairs={{0,28},{2,30},{4,0},{6,2},{8,4},{10,6},{12,8},{14,10},{16,12},{18,... | collective-permute-start | bytes 393224 | tf_op jit(solution)/shard_map/ppermute | solution.py:30
  84.6 7.0 %collective-permute-start.14 = (bf16[1,8,64,128]{3,2,1,0:T(8,128)(2,1)S(1)}, bf16[1,8,64,128]{3,2,1,0:T(8,128)(2,1)S(1)}, u32[]{:S(2)}, u32[]{:S(2)}) collective-permute-start(bf16[1,8,64,128]{3,2,1,0:T(8,128)(2,1)S(1)} %get-tuple-element.176), channel_id=1, source_target_pairs={{0,30},{2,0},{4,2},{6,4},{8,6},{10,8},{12,10},{14,12},{16,14},{18,... | collective-permute-start | bytes 393224 | tf_op jit(solution)/shard_map/ppermute | solution.py:30
  94.8 49.4 %copy-start.6 = (f32[1,256]{1,0:T(1,128)S(1)}, f32[1,256]{1,0:T(1,128)}, u32[]{:S(2)}) copy-start(f32[1,256]{1,0:T(1,128)} %param.19) | copy-start | bytes 3076
  218.0 14.4 %all-to-all-start.1 = ((f32[16,8,128]{2,1,0:T(8,128)}), f32[16,8,128]{2,1,0:T(8,128)S(1)}, u32[]{:S(2)}, u32[]{:S(2)}) async-start(f32[16,8,128]{2,1,0:T(8,128)} %bitcast.53), calls=%async_computation.1 | async-start | bytes 131072 | tf_op jit(solution)/shard_map/all_to_all | solution.py:120
Sparse Core Ops, SparseCore 0:
  120.8 23.3 all-reduce.2
